TPU v7x, 256 devices: a whole 4x4x8 slice. The times are simulated.
256 devices in a mesh: row: 4 (over y), col: 32 (over x_lo, z, core), feat: 2 (over x_hi).
Axes of the slice: x: 4 (x_hi: 2, x_lo: 2; x = x_hi * 2 + x_lo), y: 4, z: 8, core: 2. Of those that a mesh axis runs over, the one named last changes fastest.
Arguments:
- panel_student: bfloat16 [2048, 4096], P('row', 'feat'), may hold values from -0.01171875 to 0.01171875
- panel_teacher: bfloat16 [2048, 4096], P('row', 'feat'), may hold values from -0.01171875 to 0.01171875
- tokens_student: bfloat16 [24576, 4096], P('col', 'feat'), may hold values from -0.01171875 to 0.01171875
- tokens_teacher: bfloat16 [24576, 4096], P('col', 'feat'), may hold values from -0.01171875 to 0.01171875
Outputs:
- row_loss: float32 [2048], P(('row', 'col'))
- grad_panel: bfloat16 [2048, 4096], P(('row', 'col'), 'feat')
- grad_tokens: bfloat16 [24576, 4096], P('col', 'feat')
All inputs are finite; a program needn't handle non-finite values.
Results may differ from a plain program's by a relative error of at most 0.0058.
Values may be sent and summed in bfloat16 or wider, within the bound.
No kernel may reach another device: no remote copies, remote signals or barrier semaphores. Data moves between devices by JAX's collectives and lax.ppermute only.
A program may use at most 128 MiB of HBM per device.

v0:
```python
import jax
import jax.numpy as jnp
from jax import lax
from jax.sharding import PartitionSpec as P

epsilon = 1e-06


def squares(features):
    values = features.astype(jnp.float32)
    return jnp.sum(values * values, axis=1)


def inner(left, right):
    return jnp.einsum("rd,cd->rc", left, right, preferred_element_type=jnp.float32)


def inverse(total):
    return 1.0 / jnp.sqrt(total + epsilon)


def local(panel_student, panel_teacher, tokens_student, tokens_teacher):
    student_dots, teacher_dots, sq_ps, sq_pt, sq_ts, sq_tt = lax.psum(
        (
            inner(panel_student, tokens_student),
            inner(panel_teacher, tokens_teacher),
            squares(panel_student),
            squares(panel_teacher),
            squares(tokens_student),
            squares(tokens_teacher),
        ),
        "feat",
    )
    inv_ps = inverse(sq_ps)
    inv_pt = inverse(sq_pt)
    inv_ts = inverse(sq_ts)
    inv_tt = inverse(sq_tt)
    student_gram = student_dots * inv_ps[:, None] * inv_ts[None, :]
    teacher_gram = teacher_dots * inv_pt[:, None] * inv_tt[None, :]
    mismatch = student_gram - teacher_gram
    loss_part = jnp.sum(mismatch * mismatch, axis=1)
    doubled = (2.0 * mismatch).astype(jnp.bfloat16)
    panel_unit = panel_student.astype(jnp.float32) * inv_ps[:, None]
    token_unit = tokens_student.astype(jnp.float32) * inv_ts[:, None]
    panel_half = panel_unit.astype(jnp.bfloat16)
    token_half = token_unit.astype(jnp.bfloat16)
    panel_part = jnp.dot(doubled, token_half, preferred_element_type=jnp.float32)
    panel_term, row_loss = (
        lax.psum_scatter(panel_part, "col", scatter_dimension=0, tiled=True),
        lax.psum_scatter(loss_part, "col", scatter_dimension=0, tiled=True),
    )
    token_part = jnp.einsum("rc,rd->cd", doubled, panel_half, preferred_element_type=jnp.float32)
    token_term = lax.psum(token_part, "row")
    share = panel_student.shape[0] // lax.axis_size("col")
    offset = lax.axis_index("col") * share
    unit_rows = lax.dynamic_slice_in_dim(panel_unit, offset, share, 0)
    inv_rows = lax.dynamic_slice_in_dim(inv_ps, offset, share, 0)
    along_panel, along_tokens = lax.psum(
        (jnp.sum(unit_rows * panel_term, axis=1), jnp.sum(token_unit * token_term, axis=1)), "feat"
    )
    grad_panel = ((panel_term - unit_rows * along_panel[:, None]) * inv_rows[:, None]).astype(
        jnp.bfloat16
    )
    grad_tokens = ((token_term - token_unit * along_tokens[:, None]) * inv_ts[:, None]).astype(
        jnp.bfloat16
    )
    return (row_loss, grad_panel, grad_tokens)


def solution(mesh):
    placed = (P("row", "feat"), P("row", "feat"), P("col", "feat"), P("col", "feat"))
    return jax.shard_map(
        local,
        mesh=mesh,
        in_specs=placed,
        out_specs=(P(("row", "col")), P(("row", "col"), "feat"), P("col", "feat")),
        check_vma=False,
    )
```

profile of v0, /device:TPU:8, one launch (start us, length us, event | category | flops | bytes accessed | tf_op | source)
XLA Modules:
  0.0 405.1 jit_solution(3159031561422616562)
XLA Ops:
  7.2 0.0 copy-start
  7.2 0.0 all-reduce.9.cloned.1.call-start
  7.2 0.0 copy-start.1
  7.2 5.7 %fusion.17 = f32[512,768]{1,0:T(8,128)} fusion(bf16[512,2048]{1,0:T(8,128)(2,1)} %param.5, bf16[768,2048]{1,0:T(8,128)(2,1)} %param.7), kind=kOutput, calls=%fused_computation.31 | convolution fusion | flops 1610612736 | bytes 6815744 | tf_op jit(solution)/shard_map/rd,cd->rc/dot_general | solution.py:15
  12.9 0.0 copy-done
  12.9 0.0 copy-done.1
  12.9 3.1 fusion.16
  15.9 0.0 all-reduce.9.cloned.1.call-update
  16.0 0.0 all-reduce.7.cloned.1.call-start
  16.0 0.0 copy-start.2
  16.0 2.2 multiply_reduce_fusion.1
  18.3 0.0 copy-done.2
  18.3 0.5 fusion.8
  18.7 2.6 multiply_reduce_fusion
  21.3 0.7 fusion.7
  22.0 11.1 %all-reduce.2 = (f32[768]{0:T(1024)S(1)}, f32[512]{0:T(512)S(1)}, f32[768]{0:T(1024)S(1)}, f32[512]{0:T(512)S(1)}) all-reduce(f32[768]{0:T(1024)S(1)} %multiply_reduce_fusion, f32[512]{0:T(512)S(1)} %multiply_reduce_fusion.1, f32[768]{0:T(1024)S(1)} %fusion.7, f32[512]{0:T(512)S(1)} %fusion.8), channel_id=1, replica_groups=mesh['row'=4,'col'=32,'feat'=2] {'feat'}, use_global_device_ids=true, to_apply=%region_9.0 | all-reduce | flops 2560 | bytes 20480 | tf_op jit(solution)/shard_map/psum | solution.py:23
  33.1 85.0 %all-reduce.9.cloned.1.call-done = (f32[512,768]{1,0:T(8,128)}, f32[512,768]{1,0:T(8,128)}) async-done(((f32[512,768]{1,0:T(8,128)}, f32[512,768]{1,0:T(8,128)}), (f32[512,768]{1,0:T(8,128)}, f32[512,768]{1,0:T(8,128)})) %all-reduce.9.cloned.1.call-update) | async-done | bytes 3145744 | tf_op jit(solution)/shard_map/psum | solution.py:23
  118.1 0.0 copy-start.3
  118.1 2.6 multiply_reduce_fusion.2
  120.8 0.0 copy-start.4
  120.8 1.1 copy-done.4
  121.9 0.0 copy-done.3
  121.9 4.6 %fusion.12 = f32[768,2048]{1,0:T(8,128)} fusion(f32[512,768]{1,0:T(8,128)S(1)} %get-tuple-element.12, bf16[512,2048]{1,0:T(8,128)(2,1)S(1)} %copy-done.3, f32[512]{0:T(512)S(1)} %get-tuple-element.16), kind=kOutput, calls=%fused_computation.17 | convolution fusion | flops 1614544896 | bytes 9963520 | tf_op jit(solution)/shard_map/rc,rd->cd/dot_general | solution.py:52
  126.5 0.0 all-reduce.7.cloned.1.call-update
  126.5 0.0 reduce-scatter.2.cloned.1.call-start
  126.6 5.2 %fusion.9 = f32[512,2048]{1,0:T(8,128)} fusion(bf16[768,2048]{1,0:T(8,128)(2,1)S(1)} %copy-done, f32[768]{0:T(1024)S(1)} %get-tuple-element.14, f32[512,768]{1,0:T(8,128)} %copy-done.4), kind=kOutput, calls=%fused_computation.15 | convolution fusion | flops 1616117760 | bytes 8915968 | tf_op jit(solution)/shard_map/dot_general | solution.py:47
  131.8 0.0 copy-start.6
  131.8 0.0 reduce-scatter.2.cloned.1.call-update
  131.9 0.1 dynamic_slice.7
  131.9 0.6 copy-done.6
  132.5 0.6 dynamic-slice
  133.7 4.4 %convert_multiply_fusion.2 = f32[512,2048]{1,0:T(8,128)} fusion(bf16[512,2048]{1,0:T(8,128)(2,1)} %param.4, f32[512]{0:T(512)S(1)} %get-tuple-element.16), kind=kLoop, calls=%fused_computation.11 | loop fusion | flops 2097152 | bytes 6293504 | tf_op jit(solution)/shard_map/mul | solution.py:43
  138.2 55.0 %all-reduce = f32[512]{0:T(512)S(1)} all-reduce(f32[512]{0:T(512)S(1)} %get-tuple-element.11), channel_id=2, replica_groups=mesh['row'=4,'col'=32,'feat'=2] {'col'}, use_global_device_ids=true, to_apply=%region_11.0.clone | all-reduce | flops 512 | bytes 4096
  193.2 0.6 dynamic-slice.1
  193.8 63.3 %all-reduce.7.cloned.1.call-done = f32[768,2048]{1,0:T(8,128)} async-done(((f32[768,2048]{1,0:T(8,128)}), f32[768,2048]{1,0:T(8,128)}) %all-reduce.7.cloned.1.call-update) | async-done | bytes 6291472 | tf_op jit(solution)/shard_map/psum | solution.py:53
  257.1 3.7 fusion.3
  260.9 123.8 %reduce-scatter.2.cloned.1.call-done = f32[16,2048]{1,0:T(8,128)} async-done(((f32[512,2048]{1,0:T(8,128)}), f32[16,2048]{1,0:T(8,128)}) %reduce-scatter.2.cloned.1.call-update) | async-done | bytes 131088 | tf_op jit(solution)/shard_map/reduce_scatter | solution.py:49
  384.7 1.1 multiply_reduce_fusion.3
  385.8 6.5 %all-reduce.1 = (f32[16]{0:T(128)S(1)}, f32[768]{0:T(1024)S(1)}) all-reduce(f32[16]{0:T(128)S(1)} %multiply_reduce_fusion.3, f32[768]{0:T(1024)S(1)} %fusion.3), channel_id=1, replica_groups=mesh['row'=4,'col'=32,'feat'=2] {'feat'}, use_global_device_ids=true, to_apply=%region_14.0 | all-reduce | flops 784 | bytes 6272 | tf_op jit(solution)/shard_map/psum | solution.py:58
  392.3 0.0 copy-start.5
  392.3 4.7 %fusion.6 = bf16[768,2048]{1,0:T(8,128)(2,1)} fusion(f32[768,2048]{1,0:T(8,128)} %all-reduce.7.cloned.1.call-done, bf16[768,2048]{1,0:T(8,128)(2,1)S(1)} %copy-done, f32[768]{0:T(1024)S(1)} %get-tuple-element.4, f32[768]{0:T(1024)S(1)} %get-tuple-element.14), kind=kLoop, calls=%fused_computation.8 | loop fusion | flops 9437184 | bytes 12589056 | tf_op jit(solution)/shard_map/convert_element_type | solution.py:64
  397.0 0.0 copy-done.5
  397.0 1.6 multiply_convert_fusion.3
  (2 shorter events, 0.0 us)
Async XLA Ops:
  7.2 5.7 %copy-start = (bf16[768,2048]{1,0:T(8,128)(2,1)S(1)}, bf16[768,2048]{1,0:T(8,128)(2,1)}, u32[]{:S(2)}) copy-start(bf16[768,2048]{1,0:T(8,128)(2,1)} %param.6) | copy-start | bytes 9437188
  7.2 111.0 %all-reduce.9.cloned.1.call-start = ((), (), s32[]{:S(2)}) async-start(), calls=%async_computation.3 | async-start | bytes 6291456 | tf_op jit(solution)/shard_map/psum | solution.py:23
  7.2 5.7 %copy-start.1 = (bf16[512,2048]{1,0:T(8,128)(2,1)S(1)}, bf16[512,2048]{1,0:T(8,128)(2,1)}, u32[]{:S(2)}) copy-start(bf16[512,2048]{1,0:T(8,128)(2,1)} %param.4) | copy-start | bytes 6291460
  16.0 241.1 %all-reduce.7.cloned.1.call-start = ((), (), s32[]{:S(2)}) async-start(), calls=%async_computation.2 | async-start | bytes 12582912 | tf_op jit(solution)/shard_map/psum | solution.py:53
  16.0 2.2 copy-start.2
  118.1 3.8 copy-start.3
  120.8 1.1 copy-start.4
  126.5 258.1 %reduce-scatter.2.cloned.1.call-start = ((), (), s32[]{:S(2)}) async-start(), calls=%async_computation.1 | async-start | bytes 4325376 | tf_op jit(solution)/shard_map/reduce_scatter | solution.py:49
  131.8 0.7 copy-start.6
  392.3 4.7 %copy-start.5 = (f32[16,2048]{1,0:T(8,128)S(1)}, f32[16,2048]{1,0:T(8,128)}, u32[]{:S(2)}) copy-start(f32[16,2048]{1,0:T(8,128)} %reduce-scatter.2.cloned.1.call-done) | copy-start | bytes 393220
Sparse Core Ops, SparseCore 0:
  16.1 101.9 all-reduce.8
  126.7 130.4 all-reduce.6
  259.7 124.9 reduce-scatter.1
where the time goes:
time: 405 us
  waiting for transfers between devices  272 us (67%)
  blocking collectives  72.6 us (18%)
  other arithmetic  24.2 us (6%)
  matrix products  18.5 us (5%)
  between operations  14.5 us (4%)
    reduce_scatter x1, waiting for transfers between devices, local(): lax.psum_scatter(panel_part, 'col', scatter_dimension=0, tiled=True)  124 us
    psum x1, waiting for transfers between devices, local(): lax.psum((inner(panel_student, tokens_student), inner(panel_teacher, toke...  85 us
    psum x1, waiting for transfers between devices, local(): token_term = lax.psum(token_part, 'row')  63.3 us
    unnamed x1, blocking collectives  55 us
    psum x1, blocking collectives, local(): lax.psum((inner(panel_student, tokens_student), inner(panel_teacher, toke...  11.1 us
    dot_general x2, matrix products, inner(): jnp.einsum('rd,cd->rc', left, right, preferred_element_type=jnp.float32)  8.71 us
  transfers between devices with their start and end apart: 3, of which 3 were waited for; matrix products, arithmetic and copies ran while one was open for 5% of the time, Pallas kernels for 0%

commit v1 on v0

--- a/solution.py
+++ b/solution.py
@@ -50,7 +50,8 @@
         lax.psum_scatter(loss_part, "col", scatter_dimension=0, tiled=True),
     )
     token_part = jnp.einsum("rc,rd->cd", doubled, panel_half, preferred_element_type=jnp.float32)
-    token_term = lax.psum(token_part, "row")
+    parts = lax.all_gather(token_part, "row", axis=0, tiled=False)
+    token_term = parts.sum(axis=0)
     share = panel_student.shape[0] // lax.axis_size("col")
     offset = lax.axis_index("col") * share
     unit_rows = lax.dynamic_slice_in_dim(panel_unit, offset, share, 0)

time: 405 us -> 509 us (1.26)
  waiting for transfers between devices: 272 us -> 362 us
  other arithmetic: 24.2 us -> 36 us
    all_gather x0 -> x1, waiting for transfers between devices: none -> 222 us  [local(): parts = lax.all_gather(token_part, 'row', axis=0, tiled=False)]
    reduce_scatter x1, waiting for transfers between devices: 124 us -> 54.6 us  [local(): lax.psum_scatter(panel_part, 'col', scatter_dimension=0, tiled=True)]
    psum x1 -> x0, waiting for transfers between devices: 63.3 us -> none  [local(): token_term = lax.psum(token_part, 'row')]
    reduce_sum x0 -> x1, other arithmetic: none -> 12.5 us  [local(): token_term = parts.sum(axis=0)]
  transfers between devices with their start and end apart: 3 -> 3, of which waited for: 3 -> 3; matrix products, arithmetic and copies ran while one was open for 5% -> 4% of each run, Pallas kernels for 0% -> 0%
where the time goes in v1:
time: 509 us; the launch traced here: 508 us
  waiting for transfers between devices  362 us (71%)
  blocking collectives  73.4 us (14%)
  other arithmetic  36 us (7%)
  matrix products  19.3 us (4%)
  between operations  14.5 us (3%)
    all_gather x1, waiting for transfers between devices, local(): parts = lax.all_gather(token_part, 'row', axis=0, tiled=False)  222 us
    psum x1, waiting for transfers between devices, local(): lax.psum((inner(panel_student, tokens_student), inner(panel_teacher, toke...  85 us
    unnamed x1, blocking collectives  55.8 us
    reduce_scatter x1, waiting for transfers between devices, local(): lax.psum_scatter(panel_part, 'col', scatter_dimension=0, tiled=True)  54.6 us
    reduce_sum x1, other arithmetic, local(): token_term = parts.sum(axis=0)  12.5 us
    psum x1, blocking collectives, local(): lax.psum((inner(panel_student, tokens_student), inner(panel_teacher, toke...  11.1 us
  transfers between devices with their start and end apart: 3, of which 3 were waited for; matrix products, arithmetic and copies ran while one was open for 4% of the time, Pallas kernels for 0%

profile of v1, /device:TPU:8, one launch (start us, length us, event | category | flops | bytes accessed | tf_op | source)
XLA Modules:
  0.0 508.4 jit_solution(18312923789142842105)
XLA Ops:
  7.2 0.0 copy-start
  7.2 0.0 all-reduce.6.cloned.1.call-start
  7.2 0.0 copy-start.1
  7.2 5.6 %fusion.17 = f32[512,768]{1,0:T(8,128)} fusion(bf16[512,2048]{1,0:T(8,128)(2,1)} %param.5, bf16[768,2048]{1,0:T(8,128)(2,1)} %param.7), kind=kOutput, calls=%fused_computation.31 | convolution fusion | flops 1610612736 | bytes 6815744 | tf_op jit(solution)/shard_map/rd,cd->rc/dot_general | solution.py:15
  12.9 0.0 copy-done
  12.9 0.0 copy-done.1
  12.9 3.1 fusion.16
  15.9 0.0 all-reduce.6.cloned.1.call-update
  16.0 0.0 reduce-scatter.2.cloned.1.call-start
  16.0 0.0 copy-start.2
  16.0 2.2 multiply_reduce_fusion.1
  18.3 0.0 copy-done.2
  18.3 0.5 fusion.8
  18.7 2.6 multiply_reduce_fusion
  21.3 0.7 fusion.7
  22.0 11.1 %all-reduce.2 = (f32[768]{0:T(1024)S(1)}, f32[512]{0:T(512)S(1)}, f32[768]{0:T(1024)S(1)}, f32[512]{0:T(512)S(1)}) all-reduce(f32[768]{0:T(1024)S(1)} %multiply_reduce_fusion, f32[512]{0:T(512)S(1)} %multiply_reduce_fusion.1, f32[768]{0:T(1024)S(1)} %fusion.7, f32[512]{0:T(512)S(1)} %fusion.8), channel_id=1, replica_groups=mesh['row'=4,'col'=32,'feat'=2] {'feat'}, use_global_device_ids=true, to_apply=%region_9.0 | all-reduce | flops 2560 | bytes 20480 | tf_op jit(solution)/shard_map/psum | solution.py:23
  33.1 85.0 %all-reduce.6.cloned.1.call-done = (f32[512,768]{1,0:T(8,128)}, f32[512,768]{1,0:T(8,128)}) async-done(((f32[512,768]{1,0:T(8,128)}, f32[512,768]{1,0:T(8,128)}), (f32[512,768]{1,0:T(8,128)}, f32[512,768]{1,0:T(8,128)})) %all-reduce.6.cloned.1.call-update) | async-done | bytes 3145744 | tf_op jit(solution)/shard_map/psum | solution.py:23
  118.2 2.5 multiply_reduce_fusion.2
  120.6 0.0 copy-start.3
  120.6 1.1 copy-done.3
  121.8 3.9 fusion.9
  125.7 0.0 reduce-scatter.2.cloned.1.call-update
  125.7 0.0 all-gather.3.cloned.1.call-start
  125.7 6.7 %fusion.12 = f32[768,2048]{1,0:T(8,128)} fusion(f32[512,768]{1,0:T(8,128)} %copy-done.3, bf16[512,2048]{1,0:T(8,128)(2,1)} %param.4, f32[512]{0:T(512)S(1)} %get-tuple-element.16), kind=kOutput, calls=%fused_computation.17 | convolution fusion | flops 1614544896 | bytes 9963520 | tf_op jit(solution)/shard_map/rc,rd->cd/dot_general | solution.py:52
  132.5 0.0 copy-start.5
  132.5 0.0 all-gather.3.cloned.1.call-update
  132.5 0.1 dynamic_slice.7
  132.6 0.6 copy-done.5
  133.1 0.6 dynamic-slice
  134.4 3.9 convert_multiply_fusion.2
  138.3 55.8 %all-reduce = f32[512]{0:T(512)S(1)} all-reduce(f32[512]{0:T(512)S(1)} %get-tuple-element.11), channel_id=3, replica_groups=mesh['row'=4,'col'=32,'feat'=2] {'col'}, use_global_device_ids=true, to_apply=%region_11.0.clone | all-reduce | flops 512 | bytes 4096
  194.1 0.6 dynamic-slice.1
  194.7 54.6 %reduce-scatter.2.cloned.1.call-done = f32[16,2048]{1,0:T(8,128)} async-done(((f32[512,2048]{1,0:T(8,128)}), f32[16,2048]{1,0:T(8,128)}) %reduce-scatter.2.cloned.1.call-update) | async-done | bytes 131088 | tf_op jit(solution)/shard_map/reduce_scatter | solution.py:49
  249.3 1.1 multiply_reduce_fusion.3
  250.4 222.4 %all-gather.3.cloned.1.call-done = f32[3072,2048]{1,0:T(8,128)} async-done(((f32[768,2048]{1,0:T(8,128)}), f32[3072,2048]{1,0:T(8,128)}) %all-gather.3.cloned.1.call-update) | async-done | bytes 25165840 | tf_op jit(solution)/shard_map/all_gather | solution.py:53
  472.8 12.5 %reduce_sum.78 = f32[768,2048]{1,0:T(8,128)} reduce(f32[4,768,2048]{2,1,0:T(8,128)} %bitcast.6, f32[]{:T(128)} %constant.8.clone.1), dimensions={0}, to_apply=%region_15.0 | reduce | flops 4718592 | bytes 31457284 | tf_op jit(solution)/shard_map/reduce_sum | solution.py:54
  485.3 3.7 fusion.3
  489.0 6.5 %all-reduce.1 = (f32[16]{0:T(128)S(1)}, f32[768]{0:T(1024)S(1)}) all-reduce(f32[16]{0:T(128)S(1)} %multiply_reduce_fusion.3, f32[768]{0:T(1024)S(1)} %fusion.3), channel_id=1, replica_groups=mesh['row'=4,'col'=32,'feat'=2] {'feat'}, use_global_device_ids=true, to_apply=%region_14.0 | all-reduce | flops 784 | bytes 6272 | tf_op jit(solution)/shard_map/psum | solution.py:59
  495.5 0.0 copy-start.4
  495.5 4.7 fusion.6
  500.2 0.0 copy-done.4
  500.2 1.6 multiply_convert_fusion.3
  (2 shorter events, 0.0 us)
Async XLA Ops:
  7.2 5.7 %copy-start = (bf16[768,2048]{1,0:T(8,128)(2,1)S(1)}, bf16[768,2048]{1,0:T(8,128)(2,1)}, u32[]{:S(2)}) copy-start(bf16[768,2048]{1,0:T(8,128)(2,1)} %param.6) | copy-start | bytes 9437188
  7.2 111.0 %all-reduce.6.cloned.1.call-start = ((), (), s32[]{:S(2)}) async-start(), calls=%async_computation.3 | async-start | bytes 6291456 | tf_op jit(solution)/shard_map/psum | solution.py:23
  7.2 5.7 %copy-start.1 = (bf16[512,2048]{1,0:T(8,128)(2,1)S(1)}, bf16[512,2048]{1,0:T(8,128)(2,1)}, u32[]{:S(2)}) copy-start(bf16[512,2048]{1,0:T(8,128)(2,1)} %param.4) | copy-start | bytes 6291460
  16.0 233.4 %reduce-scatter.2.cloned.1.call-start = ((), (), s32[]{:S(2)}) async-start(), calls=%async_computation.1 | async-start | bytes 4325376 | tf_op jit(solution)/shard_map/reduce_scatter | solution.py:49
  16.0 2.2 copy-start.2
  120.6 1.1 copy-start.3
  125.7 347.1 %all-gather.3.cloned.1.call-start = ((), (), s32[]{:S(2)}) async-start(), calls=%async_computation.2 | async-start | bytes 31457280 | tf_op jit(solution)/shard_map/all_gather | solution.py:53
  132.5 0.7 copy-start.5
  495.5 4.7 copy-start.4
Sparse Core Ops, SparseCore 0:
  16.1 102.0 all-reduce.5
  125.8 123.4 reduce-scatter.1
  251.1 221.5 all-gather.2
